TPU v7x, 32 devices: a whole 2x2x4 slice. The times are simulated.
32 devices in a mesh: gy: 8 (over z, core), gz: 4 (over y, x).
Axes of the slice: x: 2, y: 2, z: 4, core: 2. Of those that a mesh axis runs over, the one named last changes fastest.
Arguments:
- measured: float32 [4, 1024, 1024], P('gz', 'gy'), may hold values from -20 to 20
- point_spread: float32 [1024, 1024], P('gy'), may hold values from -0.005859375 to 0.005859375
- stencil_weights: float32 [3, 3, 3], replicated, may hold values from -0.9 to 0.9
- upstream: float32 [4, 1024, 1024], P('gz', 'gy'), may hold values from -6 to 6
Outputs:
- grad_measured: float32 [4, 1024, 1024], P('gz', 'gy')
- grad_stencil: float32 [3, 3, 3], replicated
All inputs are finite; a program needn't handle non-finite values.
Results may differ from a plain program's by a relative error of at most 0.00021.
Values sent between devices are 32-bit elements; how exact they have to be, the bound alone decides.
A program may use at most 64 MiB of HBM per device.

v0:
```python
import math

import jax
import jax.numpy as jnp
from jax import lax
from jax.sharding import PartitionSpec as P

ITERS = 2


highest = lax.Precision.HIGHEST


def extended(value, sides, width):
    for axis, dim in sides:
        size, length = (lax.axis_size(axis), value.shape[dim])
        up = [(i, (i + 1) % size) for i in range(size - 1)]
        down = [(j, i) for i, j in up]
        last = lax.slice_in_dim(value, length - width, length, axis=dim)
        first = lax.slice_in_dim(value, 0, width, axis=dim)
        before = lax.ppermute(last, axis, up)
        after = lax.ppermute(first, axis, down)
        value = jnp.concatenate([before, value, after], axis=dim)
    return value


def waves(count_first, count_second, length):
    product = (
        jnp.arange(count_first, dtype=jnp.int32)[:, None]
        * jnp.arange(count_second, dtype=jnp.int32)[None, :]
        % length
    )
    angle = product.astype(jnp.float32) * (2.0 * math.pi / length)
    return (jnp.cos(angle), jnp.sin(angle))


def contract(form, left, table):
    return jnp.einsum(form, left, table, precision=highest)


def forward_block(cosine, sine):
    return jnp.stack([jnp.stack([cosine, -sine], 1), jnp.stack([sine, cosine], 1)], 0)


def inverse_block(cosine, sine):
    return jnp.stack([jnp.stack([cosine, sine], 1), jnp.stack([-sine, cosine], 1)], 0)


def build_tables(columns, row_total):
    radix_cols = columns // 128
    radix_rows = row_total // 128
    first_cos, first_sin = waves(radix_cols, radix_cols, radix_cols)
    turn_cos, turn_sin = waves(radix_cols, 128, columns)
    inner_cos, inner_sin = waves(128, 128, 128)
    second_cos, second_sin = waves(radix_rows, radix_rows, radix_rows)
    spin_cos, spin_sin = waves(radix_rows, 128, row_total)
    first_start = jnp.stack([first_cos, -first_sin], 1)
    first_final = jnp.stack([first_cos, -first_sin], 0)
    return (
        first_start,
        first_final,
        turn_cos,
        turn_sin,
        forward_block(inner_cos, inner_sin),
        inverse_block(inner_cos, inner_sin),
        forward_block(second_cos, second_sin),
        inverse_block(second_cos, second_sin),
        spin_cos,
        spin_sin,
    )


def forward_fourier_map(volume, twiddle_tables):
    (
        first_start,
        first_final,
        turn_cos,
        turn_sin,
        inner_fwd,
        inner_inv,
        second_fwd,
        second_inv,
        spin_cos,
        spin_sin,
    ) = twiddle_tables
    batches, planes, row_count, columns = volume.shape
    groups = lax.axis_size("gy")
    per_group = 128 // row_count
    bins_here = columns // groups
    radix_cols = first_start.shape[0]
    radix_rows = second_fwd.shape[1]
    blocked = volume.reshape(batches, planes, row_count, radix_cols, 128)
    parts = contract("bzyan,adk->dbzykn", blocked, first_start)
    twisted = jnp.stack(
        [parts[0] * turn_cos + parts[1] * turn_sin, parts[1] * turn_cos - parts[0] * turn_sin], 0
    )
    across = contract("cbzykn,cndq->dbkqzy", twisted, inner_fwd)
    arrived = lax.all_to_all(
        across.reshape(2, batches, columns, planes * row_count),
        "gy",
        split_axis=2,
        concat_axis=3,
        tiled=True,
    )
    arrived = arrived.reshape(2, batches, bins_here, radix_rows, per_group, planes, row_count)
    down = contract("cbpajzy,cadk->dbpkzjy", arrived, second_fwd)
    down = down.reshape(2, batches, bins_here, radix_rows, planes, 128)
    spin_real = spin_cos[:, None, :]
    spin_imaginary = spin_sin[:, None, :]
    spun = jnp.stack(
        [
            down[0] * spin_real + down[1] * spin_imaginary,
            down[1] * spin_real - down[0] * spin_imaginary,
        ],
        0,
    )
    return contract("cbpkzm,cmdq->dbpkzq", spun, inner_fwd)


def inverse_transform(spectrum, twiddle_tables):
    (
        first_start,
        first_final,
        turn_cos,
        turn_sin,
        inner_fwd,
        inner_inv,
        second_fwd,
        second_inv,
        spin_cos,
        spin_sin,
    ) = twiddle_tables
    unused, batches, bins_here, radix_rows, planes, width = spectrum.shape
    groups = lax.axis_size("gy")
    columns = bins_here * groups
    radix_cols = first_start.shape[0]
    row_count = radix_rows * 128 // groups
    per_group = 128 // row_count
    down = contract("cbpkzq,cqdm->dbpkzm", spectrum, inner_inv)
    spin_real = spin_cos[:, None, :]
    spin_imaginary = spin_sin[:, None, :]
    twist = jnp.stack(
        [
            down[0] * spin_real - down[1] * spin_imaginary,
            down[1] * spin_real + down[0] * spin_imaginary,
        ],
        0,
    )
    twist = twist.reshape(2, batches, bins_here, radix_rows, planes, per_group, row_count)
    rows_part = contract("cbpkzjy,ckda->dbpajzy", twist, second_inv)
    arrived = lax.all_to_all(
        rows_part.reshape(2, batches, bins_here, groups * planes * row_count),
        "gy",
        split_axis=3,
        concat_axis=2,
        tiled=True,
    )
    arrived = arrived.reshape(2, batches, radix_cols, 128, planes, row_count)
    inner = contract("cbkqzy,cqdn->dbzykn", arrived, inner_inv)
    turned = jnp.stack(
        [inner[0] * turn_cos - inner[1] * turn_sin, inner[1] * turn_cos + inner[0] * turn_sin], 0
    )
    volume = contract("cbzykn,cka->bzyan", turned, first_final)
    return volume.reshape(batches, planes, row_count, columns) / float(columns * radix_rows * 128)


def filtered(volume, power_gain, twiddle_tables):
    spectrum = forward_fourier_map(volume[None], twiddle_tables)
    return inverse_transform(spectrum * power_gain, twiddle_tables)[0]


def extend(volume):
    grown = extended(volume, (("gy", 1), ("gz", 0)), 1)
    return jnp.pad(grown, ((0, 0), (0, 0), (1, 1)))


def stencil(grown, kernel, planes, row_count, columns):
    summed = jnp.zeros((planes, row_count, columns), jnp.float32)
    for shift_z in range(3):
        for shift_y in range(3):
            for shift_x in range(3):
                summed = (
                    summed
                    + kernel[shift_z, shift_y, shift_x]
                    * grown[
                        shift_z : shift_z + planes,
                        shift_y : shift_y + row_count,
                        shift_x : shift_x + columns,
                    ]
                )
    return summed


def correlate(values, grown):
    planes, row_count, columns = values.shape
    pieces = []
    for shift_z in range(3):
        for shift_y in range(3):
            for shift_x in range(3):
                pieces.append(
                    jnp.sum(
                        values
                        * grown[
                            shift_z : shift_z + planes,
                            shift_y : shift_y + row_count,
                            shift_x : shift_x + columns,
                        ]
                    )
                )
    return jnp.stack(pieces)


def regular(volume, kernel, flipped):
    planes, row_count, columns = volume.shape
    grown = extend(volume)
    mapped = stencil(grown, kernel, planes, row_count, columns)
    back = stencil(extend(mapped), flipped, planes, row_count, columns)
    return (back, grown, mapped)


def local(measured, point_spread, stencil_weights, upstream):
    planes, row_count, columns = measured.shape
    groups = lax.axis_size("gy")
    cells = planes * row_count * columns * groups * lax.axis_size("gz")
    twiddle_tables = build_tables(columns, row_count * groups)
    flipped = stencil_weights[::-1, ::-1, ::-1]
    optical = forward_fourier_map(point_spread[None, None], twiddle_tables)
    optical_real = optical[0]
    optical_imaginary = optical[1]
    power_gain = optical_real * optical_real + optical_imaginary * optical_imaginary
    observed = forward_fourier_map(measured[None], twiddle_tables)
    adjoint_spectrum = jnp.stack(
        [
            observed[0] * optical_real + observed[1] * optical_imaginary,
            observed[1] * optical_real - observed[0] * optical_imaginary,
        ],
        0,
    )
    right_side = inverse_transform(adjoint_spectrum, twiddle_tables)[0]
    directions = [right_side]
    residuals = [right_side]
    images = []
    norms = []
    curvatures = []
    step_sizes = []
    ratios = []
    grown_list = []
    mapped_list = []
    upward = []
    crossed = []
    norm_now = lax.psum(jnp.sum(right_side * right_side), ("gy", "gz"))
    for iteration in range(ITERS):
        direction = directions[iteration]
        back, grown, mapped = regular(direction, stencil_weights, flipped)
        blurred = filtered(direction, power_gain, twiddle_tables)
        applied = blurred + back
        curvature, along = lax.psum(
            (jnp.sum(direction * applied), jnp.sum(upstream * direction)), ("gy", "gz")
        )
        upward.append(along)
        step_size = norm_now / curvature
        images.append(applied)
        norms.append(norm_now)
        curvatures.append(curvature)
        step_sizes.append(step_size)
        grown_list.append(grown)
        mapped_list.append(mapped)
        if iteration + 1 < ITERS:
            residual = residuals[iteration] - step_size * applied
            norm_next, cross = lax.psum(
                (jnp.sum(residual * residual), jnp.sum(residual * applied)), ("gy", "gz")
            )
            crossed.append(cross)
            ratio = norm_next / norm_now
            ratios.append(ratio)
            residuals.append(residual)
            directions.append(residual + ratio * direction)
            norm_now = norm_next
    grad_direction = None
    grad_residual = None
    grad_norm = 0.0
    stencil_terms = jnp.zeros((27,), jnp.float32)
    for iteration in reversed(range(ITERS)):
        direction = directions[iteration]
        applied = images[iteration]
        step_size = step_sizes[iteration]
        grad_step = upward[iteration]
        grad_new = step_size * upstream
        grad_norm_here = 0.0
        grad_residual_next = None
        if iteration + 1 < ITERS:
            grad_ratio, known_image = lax.psum(
                (jnp.sum(grad_direction * direction), jnp.sum(grad_direction * applied)),
                ("gy", "gz"),
            )
            grad_norm = grad_norm + grad_ratio / norms[iteration]
            grad_image = known_image + 2.0 * grad_norm * crossed[iteration]
            grad_residual_next = grad_direction + 2.0 * grad_norm * residuals[iteration + 1]
            grad_step = grad_step - grad_image
            grad_new = grad_new + ratios[iteration] * grad_direction
            grad_norm_here = -grad_ratio * ratios[iteration] / norms[iteration]
        grad_norm_step = grad_norm_here + grad_step / curvatures[iteration]
        grad_curve = -grad_step * step_size / curvatures[iteration]
        grad_new = grad_new + 2.0 * grad_curve * applied
        mapped = mapped_list[iteration]
        grown = grown_list[iteration]
        if grad_residual_next is not None:
            back_other, grown_other, mapped_other = regular(
                grad_residual_next, stencil_weights, flipped
            )
            blurred_other = filtered(grad_residual_next, power_gain, twiddle_tables)
            grad_new = grad_new - step_size * (blurred_other + back_other)
            local_terms = correlate(
                2.0 * grad_curve * mapped - step_size * mapped_other, grown
            ) - step_size * correlate(mapped, grown_other)
        else:
            local_terms = correlate(2.0 * grad_curve * mapped, grown)
        stencil_terms = stencil_terms + local_terms
        grad_direction = grad_new
        grad_residual = grad_residual_next
        grad_norm = grad_norm_step
    stencil_terms = lax.psum(stencil_terms, ("gy", "gz"))
    grad_right = grad_direction + 2.0 * grad_norm * right_side
    grad_right = grad_right + grad_residual
    right_spectrum = forward_fourier_map(grad_right[None], twiddle_tables)
    product = jnp.stack(
        [
            right_spectrum[0] * optical_real - right_spectrum[1] * optical_imaginary,
            right_spectrum[1] * optical_real + right_spectrum[0] * optical_imaginary,
        ],
        0,
    )
    grad_measured = inverse_transform(product, twiddle_tables)[0]
    grad_stencil = stencil_terms.reshape(3, 3, 3) / math.sqrt(cells)
    return (grad_measured, grad_stencil)


def solution(mesh):
    return jax.shard_map(
        local,
        mesh=mesh,
        in_specs=(P("gz", "gy", None), P("gy", None), P(), P("gz", "gy", None)),
        out_specs=(P("gz", "gy", None), P()),
        check_vma=False,
    )
```

profile of v0, /device:TPU:0, one launch (start us, length us, event | category | flops | bytes accessed | tf_op | source)
XLA Modules:
  0.0 989.4 jit_solution(10481943100277052143)
XLA Ops:
  18.3 23.5 %all-to-all-done.1 = f32[2,1,1024,128]{3,0,1,2:T(2,128)S(1)} async-done(((f32[2,1,1024,128]{3,0,1,2:T(2,128)}), f32[2,1,1024,128]{3,0,1,2:T(2,128)S(1)}, u32[]{:S(2)}, u32[]{:S(2)}) %all-to-all-start.1) | async-done | bytes 1048608 | tf_op jit(solution)/shard_map/all_to_all | solution.py:98
  48.5 23.9 %all-to-all-done = f32[2,1,1024,128]{3,0,1,2:T(2,128)S(1)} async-done(((f32[2,1,1024,128]{3,0,1,2:T(2,128)}), f32[2,1,1024,128]{3,0,1,2:T(2,128)S(1)}, u32[]{:S(2)}, u32[]{:S(2)}) %all-to-all-start) | async-done | bytes 1048608 | tf_op jit(solution)/shard_map/all_to_all | solution.py:98
  85.5 26.4 %all-to-all-done.2 = f32[2,1,128,1024]{2,0,1,3:T(2,128)S(1)} async-done(((f32[2,1,128,1024]{2,0,1,3:T(2,128)}), f32[2,1,128,1024]{2,0,1,3:T(2,128)S(1)}, u32[]{:S(2)}, u32[]{:S(2)}) %all-to-all-start.2) | async-done | bytes 1048608 | tf_op jit(solution)/shard_map/all_to_all | solution.py:151
  161.6 20.5 %all-to-all-start.4 = ((f32[2,1,128,1024]{2,0,1,3:T(2,128)}), f32[2,1,128,1024]{2,0,1,3:T(2,128)}, u32[]{:S(2)}, u32[]{:S(2)}) async-start(f32[2,1,128,1024]{2,0,1,3:T(2,128)} %bitcast.158), calls=%async_computation.4 | async-start | bytes 2097152 | tf_op jit(solution)/shard_map/all_to_all | solution.py:151
  183.5 18.5 %multiply_add_fusion.17 = f32[1,128,1024]{2,1,0:T(8,128)S(1)} fusion(f32[1,128,1024]{2,1,0:T(8,128)S(1)} %copy-done.55, f32[3,130,1026]{2,1,0:T(8,128)S(1)} %select_maximum_fusion.20, f32[1,130,1024]{2,1,0:T(8,128)S(1)} %copy.424, f32[1,130,1024]{2,1,0:T(8,128)S(1)} %copy.423, f32[1,128,1024]{2,1,0:T(8,128)S(1)} %div.80, f32[1,1,1024]{2,1,0:T(1,128)S(1)} %copy-done.75, ...), kind=kLoop, calls=%fused_computation.483 | loop fusion | flops 7077888 | bytes 14164072 | tf_op jit(solution)/shard_map/add | solution.py:183
  218.0 8.9 collective-permute-done.7
  242.3 26.9 %multiply_reduce_fusion.88 = (f32[]{:T(128)}, f32[1,128,1024]{2,1,0:T(8,128)}) fusion(f32[1,128,1024]{2,1,0:T(8,128)S(1)} %div.80, f32[1,128,1024]{2,1,0:T(8,128)} %div.84, f32[3,130,1026]{2,1,0:T(8,128)} %select_maximum_fusion.16, f32[]{:T(128)} %bitcast.174, f32[1,130,1024]{2,1,0:T(8,128)} %copy-done.43, f32[]{:T(128)} %bitcast.175, f32[]{:T(128)} %bitcast.176, ...), kind=kLoop, calls=%fused_computation.482 | loop fusion | flops 7602175 | bytes 14688368 | tf_op jit(solution)/shard_map/reduce_sum | solution.py:258
  269.2 52.7 %all-reduce.8 = (f32[]{:T(128)}, f32[]{:T(128)}) all-reduce(f32[]{:T(128)} %get-tuple-element.229, f32[]{:T(128)} %get-tuple-element.121), channel_id=1, replica_groups=mesh['gy'=8,'gz'=4] {'gy','gz'}, use_global_device_ids=true, to_apply=%region_1.2 | all-reduce | flops 2 | bytes 16 | tf_op jit(solution)/shard_map/psum | solution.py:251
  325.9 39.0 %psum.72 = f32[]{:T(128)} all-reduce(f32[]{:T(128)} %get-tuple-element.119), channel_id=1, replica_groups=mesh['gy'=8,'gz'=4] {'gy','gz'}, use_global_device_ids=true, to_apply=%region_5.6 | all-reduce | flops 1 | bytes 8 | tf_op jit(solution)/shard_map/psum | solution.py:270
  423.8 23.4 %all-to-all-start.6 = ((f32[2,1,128,1024]{2,0,1,3:T(2,128)}), f32[2,1,128,1024]{2,0,1,3:T(2,128)}, u32[]{:S(2)}, u32[]{:S(2)}) async-start(f32[2,1,128,1024]{2,0,1,3:T(2,128)} %bitcast.927), calls=%async_computation.6 | async-start | bytes 2097152 | tf_op jit(solution)/shard_map/all_to_all | solution.py:151
  449.4 19.1 %multiply_add_fusion.12 = f32[1,128,1024]{2,1,0:T(8,128)S(1)} fusion(f32[1,128,1024]{2,1,0:T(8,128)S(1)} %copy-done.17, f32[3,130,1026]{2,1,0:T(8,128)S(1)} %select_maximum_fusion.12, f32[1,130,1024]{2,1,0:T(8,128)S(1)} %copy-done.7, f32[1,130,1024]{2,1,0:T(8,128)S(1)} %copy-done.9, f32[1,1,1024]{2,1,0:T(1,128)S(1)} %copy-done.79, ...), kind=kLoop, calls=%fused_computation.470 | loop fusion | flops 7208960 | bytes 13639788 | tf_op jit(solution)/shard_map/add | solution.py:183
  484.4 9.1 collective-permute-done.15
  508.8 27.4 %multiply_reduce_fusion.86 = (f32[]{:T(128)}, f32[]{:T(128)}, f32[1,128,1024]{2,1,0:T(8,128)}) fusion(f32[1,128,1024]{2,1,0:T(8,128)} %copy-done.16, f32[1,128,1024]{2,1,0:T(8,128)} %param.7, f32[1,128,1024]{2,1,0:T(8,128)} %div.90, f32[3,130,1026]{2,1,0:T(8,128)} %select_maximum_fusion.8, f32[]{:T(128)} %bitcast.174, f32[1,130,1024]{2,1,0:T(8,128)} %copy-done.42, ...), kind=kLoop, calls=%fused_computation.469 | loop fusion | flops 7864318 | bytes 15212660 | tf_op jit(solution)/shard_map/reduce_sum | solution.py:258
  536.1 52.7 %all-reduce.7 = (f32[]{:T(128)}, f32[]{:T(128)}) all-reduce(f32[]{:T(128)} %get-tuple-element.106, f32[]{:T(128)} %get-tuple-element.105), channel_id=1, replica_groups=mesh['gy'=8,'gz'=4] {'gy','gz'}, use_global_device_ids=true, to_apply=%region_9.10 | all-reduce | flops 2 | bytes 16 | tf_op jit(solution)/shard_map/psum | solution.py:257
  596.1 39.1 %all-reduce.6 = (f32[]{:T(128)}, f32[]{:T(128)}, f32[]{:T(128)}, f32[]{:T(128)}) all-reduce(f32[]{:T(128)} %get-tuple-element.103, f32[]{:T(128)} %get-tuple-element.104, f32[]{:T(128)} %get-tuple-element.102, f32[]{:T(128)} %get-tuple-element.101), channel_id=1, replica_groups=mesh['gy'=8,'gz'=4] {'gy','gz'}, use_global_device_ids=true, to_apply=%region_15.16 | all-reduce | flops 4 | bytes 32 | tf_op jit(solution)/shard_map/psum | solution.py:292
  691.3 27.0 %all-to-all-start.8 = ((f32[2,1,128,1024]{2,0,1,3:T(2,128)}), f32[2,1,128,1024]{2,0,1,3:T(2,128)}, u32[]{:S(2)}, u32[]{:S(2)}) async-start(f32[2,1,128,1024]{2,0,1,3:T(2,128)} %bitcast.926), calls=%async_computation.8 | async-start | bytes 2097152 | tf_op jit(solution)/shard_map/all_to_all | solution.py:151
  718.2 26.4 %multiply_reduce_fusion.28 = (f32[]{:T(128)}, f32[]{:T(128)}, f32[]{:T(128)}, f32[]{:T(128)}, f32[]{:T(128)}, /*index=5*/f32[]{:T(128)}, f32[]{:T(128)}, f32[]{:...) fusion(f32[1,130,1024]{2,1,0:T(8,128)S(1)} %copy.424, f32[1,128,1024]{2,1,0:T(8,128)S(1)} %div.80, ...), kind=kLoop, calls=%fused_computation.388 | loop fusion | flops 10223607 | bytes 18366616 | tf_op jit(solution)/shard_map/reduce_sum | solution.py:201
  754.1 7.6 collective-permute-start.22
  786.7 26.3 %fusion.84 = f32[16,8,8,128]{3,1,2,0:T(8,128)S(1)} fusion(f32[1,128,1024]{2,1,0:T(8,128)S(1)} %copy-done.15, f32[1,128,1024]{2,1,0:T(8,128)} %mul.3665, f32[1,128,1024]{2,1,0:T(8,128)} %div.99, f32[3,130,1026]{2,1,0:T(8,128)} %select_maximum_fusion, f32[1,130,1024]{2,1,0:T(8,128)S(1)} %copy.504, f32[1,1,1024]{2,1,0:T(1,128)S(1)} %collective-permute-done.21, ...), kind=kLoop, calls=%fused_computation.180 | loop fusion | flops 8519680 | bytes 16785528
  817.1 33.0 %all_to_all.165 = f32[2,1,1024,128]{3,0,1,2:T(2,128)S(1)} all-to-all(f32[2,1,1024,128]{3,0,1,2:T(2,128)S(1)} %copy.512), channel_id=1, replica_groups=mesh['gy'=8,'gz'=4] {'gy'}, dimensions={2} | all-to-all | bytes 2097152 | tf_op jit(solution)/shard_map/all_to_all | solution.py:98
  873.8 17.1 %stack.528 = f32[27]{0:T(128)S(1)} concatenate(f32[1]{0:T(128)} %bitcast.380, f32[1]{0:T(128)} %bitcast.381, f32[1]{0:T(128)} %bitcast.382, f32[1]{0:T(128)} %bitcast.383, f32[1]{0:T(128)} %bitcast.384, f32[1]{0:T(128)} %bitcast.385, f32[1]{0:T(128)} %bitcast.386, f32[1]{0:T(128)} %bitcast.387, f32[1]{0:T(128)} %bitcast.388, f32[1]{0:T(128)} %bitcast.389, f32[1]{0:T(128)} %bitcast.390, ...), dimensions={0} | concatenate | bytes 216 | tf_op jit(solution)/shard_map/stack | solution.py:210
  896.3 17.0 %stack.584 = f32[27]{0:T(128)S(1)} concatenate(f32[1]{0:T(128)} %bitcast.434, f32[1]{0:T(128)} %bitcast.435, f32[1]{0:T(128)} %bitcast.436, f32[1]{0:T(128)} %bitcast.437, f32[1]{0:T(128)} %bitcast.438, f32[1]{0:T(128)} %bitcast.439, f32[1]{0:T(128)} %bitcast.440, f32[1]{0:T(128)} %bitcast.441, f32[1]{0:T(128)} %bitcast.442, f32[1]{0:T(128)} %bitcast.443, f32[1]{0:T(128)} %bitcast.444, ...), dimensions={0} | concatenate | bytes 216 | tf_op jit(solution)/shard_map/stack | solution.py:210
  916.1 17.1 %stack.556 = f32[27]{0:T(128)S(1)} concatenate(f32[1]{0:T(128)} %bitcast.407, f32[1]{0:T(128)} %bitcast.408, f32[1]{0:T(128)} %bitcast.409, f32[1]{0:T(128)} %bitcast.410, f32[1]{0:T(128)} %bitcast.411, f32[1]{0:T(128)} %bitcast.412, f32[1]{0:T(128)} %bitcast.413, f32[1]{0:T(128)} %bitcast.414, f32[1]{0:T(128)} %bitcast.415, f32[1]{0:T(128)} %bitcast.416, f32[1]{0:T(128)} %bitcast.417, ...), dimensions={0} | concatenate | bytes 216 | tf_op jit(solution)/shard_map/stack | solution.py:210
  933.2 50.5 %psum.79 = f32[27]{0:T(128)S(1)} all-reduce(f32[27]{0:T(128)S(1)} %subtract_add_fusion), channel_id=1, replica_groups=mesh['gy'=8,'gz'=4] {'gy','gz'}, use_global_device_ids=true, to_apply=%region_99.100 | all-reduce | flops 27 | bytes 216 | tf_op jit(solution)/shard_map/psum | solution.py:322
  (429 shorter events, 339.9 us)
Async XLA Ops:
  8.9 32.9 %all-to-all-start.1 = ((f32[2,1,1024,128]{3,0,1,2:T(2,128)}), f32[2,1,1024,128]{3,0,1,2:T(2,128)S(1)}, u32[]{:S(2)}, u32[]{:S(2)}) async-start(f32[2,1,1024,128]{3,0,1,2:T(2,128)} %copy.392), calls=%async_computation.1 | async-start | bytes 2097152 | tf_op jit(solution)/shard_map/all_to_all | solution.py:98
  41.8 30.6 %all-to-all-start = ((f32[2,1,1024,128]{3,0,1,2:T(2,128)}), f32[2,1,1024,128]{3,0,1,2:T(2,128)S(1)}, u32[]{:S(2)}, u32[]{:S(2)}) async-start(f32[2,1,1024,128]{3,0,1,2:T(2,128)} %copy.386), calls=%async_computation | async-start | bytes 2097152 | tf_op jit(solution)/shard_map/all_to_all | solution.py:98
  81.7 30.2 %all-to-all-start.2 = ((f32[2,1,128,1024]{2,0,1,3:T(2,128)}), f32[2,1,128,1024]{2,0,1,3:T(2,128)S(1)}, u32[]{:S(2)}, u32[]{:S(2)}) async-start(f32[2,1,128,1024]{2,0,1,3:T(2,128)} %bitcast.96), calls=%async_computation.2 | async-start | bytes 2097152 | tf_op jit(solution)/shard_map/all_to_all | solution.py:151
  119.6 30.8 %all-to-all-start.3 = ((f32[2,1,1024,128]{3,0,1,2:T(2,128)}), f32[2,1,1024,128]{3,0,1,2:T(2,128)}, u32[]{:S(2)}, u32[]{:S(2)}) async-start(f32[2,1,1024,128]{3,0,1,2:T(2,128)} %copy.407), calls=%async_computation.3 | async-start | bytes 2097152 | tf_op jit(solution)/shard_map/all_to_all | solution.py:98
  132.5 11.3 %collective-permute-start.3 = (f32[1,130,1024]{2,0,1:T(1,128)S(1)}, f32[1,130,1024]{2,0,1:T(1,128)}, u32[]{:S(2)}, u32[]{:S(2)}) collective-permute-start(f32[1,130,1024]{2,0,1:T(1,128)S(1)} %copy.421), channel_id=1, source_target_pairs={{1,0},{2,1},{3,2},{5,4},{6,5},{7,6},{9,8},{10,9},{11,10},{13,12},{... | collective-permute-start | bytes 1597448 | tf_op jit(solution)/shard_map/ppermute | solution.py:22
  133.8 11.3 %collective-permute-start.2 = (f32[1,130,1024]{2,0,1:T(1,128)S(1)}, f32[1,130,1024]{2,0,1:T(1,128)S(1)}, u32[]{:S(2)}, u32[]{:S(2)}) collective-permute-start(f32[1,130,1024]{2,0,1:T(1,128)S(1)} %copy.421), channel_id=1, source_target_pairs={{0,1},{1,2},{2,3},{4,5},{5,6},{6,7},{8,9},{9,10},{10,11},{12,13},{... | collective-permute-start | bytes 1597448 | tf_op jit(solution)/shard_map/ppermute | solution.py:21
  161.6 69.9 %all-to-all-start.4 = ((f32[2,1,128,1024]{2,0,1,3:T(2,128)}), f32[2,1,128,1024]{2,0,1,3:T(2,128)}, u32[]{:S(2)}, u32[]{:S(2)}) async-start(f32[2,1,128,1024]{2,0,1,3:T(2,128)} %bitcast.158), calls=%async_computation.4 | async-start | bytes 2097152 | tf_op jit(solution)/shard_map/all_to_all | solution.py:151
  209.3 17.7 %collective-permute-start.7 = (f32[1,130,1024]{2,0,1:T(1,128)S(1)}, f32[1,130,1024]{2,0,1:T(1,128)S(1)}, u32[]{:S(2)}, u32[]{:S(2)}) collective-permute-start(f32[1,130,1024]{2,0,1:T(1,128)S(1)} %copy.431), channel_id=1, source_target_pairs={{1,0},{2,1},{3,2},{5,4},{6,5},{7,6},{9,8},{10,9},{11,10},{13,12},{... | collective-permute-start | bytes 1597448 | tf_op jit(solution)/shard_map/ppermute | solution.py:22
  210.6 18.1 %collective-permute-start.6 = (f32[1,130,1024]{2,0,1:T(1,128)S(1)}, f32[1,130,1024]{2,0,1:T(1,128)S(1)}, u32[]{:S(2)}, u32[]{:S(2)}) collective-permute-start(f32[1,130,1024]{2,0,1:T(1,128)S(1)} %copy.431), channel_id=1, source_target_pairs={{0,1},{1,2},{2,3},{4,5},{5,6},{6,7},{8,9},{9,10},{10,11},{12,13},{... | collective-permute-start | bytes 1597448 | tf_op jit(solution)/shard_map/ppermute | solution.py:21
  377.2 30.9 %all-to-all-start.5 = ((f32[2,1,1024,128]{3,0,1,2:T(2,128)}), f32[2,1,1024,128]{3,0,1,2:T(2,128)}, u32[]{:S(2)}, u32[]{:S(2)}) async-start(f32[2,1,1024,128]{3,0,1,2:T(2,128)} %copy.442), calls=%async_computation.5 | async-start | bytes 2097152 | tf_op jit(solution)/shard_map/all_to_all | solution.py:98
  384.5 4.3 collective-permute-start.9
  391.1 11.4 %collective-permute-start.11 = (f32[1,130,1024]{2,0,1:T(1,128)S(1)}, f32[1,130,1024]{2,0,1:T(1,128)S(1)}, u32[]{:S(2)}, u32[]{:S(2)}) collective-permute-start(f32[1,130,1024]{2,0,1:T(1,128)S(1)} %copy.456), channel_id=1, source_target_pairs={{1,0},{2,1},{3,2},{5,4},{6,5},{7,6},{9,8},{10,9},{11,10},{13,12},{... | collective-permute-start | bytes 1597448 | tf_op jit(solution)/shard_map/ppermute | solution.py:22
  392.4 11.6 %collective-permute-start.10 = (f32[1,130,1024]{2,0,1:T(1,128)S(1)}, f32[1,130,1024]{2,0,1:T(1,128)S(1)}, u32[]{:S(2)}, u32[]{:S(2)}) collective-permute-start(f32[1,130,1024]{2,0,1:T(1,128)S(1)} %copy.456), channel_id=1, source_target_pairs={{0,1},{1,2},{2,3},{4,5},{5,6},{6,7},{8,9},{9,10},{10,11},{12,13},{... | collective-permute-start | bytes 1597448 | tf_op jit(solution)/shard_map/ppermute | solution.py:21
  423.8 74.1 %all-to-all-start.6 = ((f32[2,1,128,1024]{2,0,1,3:T(2,128)}), f32[2,1,128,1024]{2,0,1,3:T(2,128)}, u32[]{:S(2)}, u32[]{:S(2)}) async-start(f32[2,1,128,1024]{2,0,1,3:T(2,128)} %bitcast.927), calls=%async_computation.6 | async-start | bytes 2097152 | tf_op jit(solution)/shard_map/all_to_all | solution.py:151
  475.8 17.7 %collective-permute-start.15 = (f32[1,130,1024]{2,0,1:T(1,128)S(1)}, f32[1,130,1024]{2,0,1:T(1,128)S(1)}, u32[]{:S(2)}, u32[]{:S(2)}) collective-permute-start(f32[1,130,1024]{2,0,1:T(1,128)S(1)} %copy.466), channel_id=1, source_target_pairs={{1,0},{2,1},{3,2},{5,4},{6,5},{7,6},{9,8},{10,9},{11,10},{13,12},{... | collective-permute-start | bytes 1597448 | tf_op jit(solution)/shard_map/ppermute | solution.py:22
  477.1 18.1 %collective-permute-start.14 = (f32[1,130,1024]{2,0,1:T(1,128)S(1)}, f32[1,130,1024]{2,0,1:T(1,128)S(1)}, u32[]{:S(2)}, u32[]{:S(2)}) collective-permute-start(f32[1,130,1024]{2,0,1:T(1,128)S(1)} %copy.466), channel_id=1, source_target_pairs={{0,1},{1,2},{2,3},{4,5},{5,6},{6,7},{8,9},{9,10},{10,11},{12,13},{... | collective-permute-start | bytes 1597448 | tf_op jit(solution)/shard_map/ppermute | solution.py:21
  643.7 31.7 %all-to-all-start.7 = ((f32[2,1,1024,128]{3,0,1,2:T(2,128)}), f32[2,1,1024,128]{3,0,1,2:T(2,128)}, u32[]{:S(2)}, u32[]{:S(2)}) async-start(f32[2,1,1024,128]{3,0,1,2:T(2,128)} %copy.477), calls=%async_computation.7 | async-start | bytes 2097152 | tf_op jit(solution)/shard_map/all_to_all | solution.py:98
  651.1 4.3 collective-permute-start.17
  658.4 11.7 %collective-permute-start.19 = (f32[1,130,1024]{2,0,1:T(1,128)}, f32[1,130,1024]{2,0,1:T(1,128)}, u32[]{:S(2)}, u32[]{:S(2)}) collective-permute-start(f32[1,130,1024]{2,0,1:T(1,128)} %copy.491), channel_id=1, source_target_pairs={{1,0},{2,1},{3,2},{5,4},{6,5},{7,6},{9,8},{10,9},{11,10},{13,12},{... | collective-permute-start | bytes 1597448 | tf_op jit(solution)/shard_map/ppermute | solution.py:22
  659.7 11.9 %collective-permute-start.18 = (f32[1,130,1024]{2,0,1:T(1,128)}, f32[1,130,1024]{2,0,1:T(1,128)}, u32[]{:S(2)}, u32[]{:S(2)}) collective-permute-start(f32[1,130,1024]{2,0,1:T(1,128)} %copy.491), channel_id=1, source_target_pairs={{0,1},{1,2},{2,3},{4,5},{5,6},{6,7},{8,9},{9,10},{10,11},{12,13},{... | collective-permute-start | bytes 1597448 | tf_op jit(solution)/shard_map/ppermute | solution.py:21
  691.3 84.7 %all-to-all-start.8 = ((f32[2,1,128,1024]{2,0,1,3:T(2,128)}), f32[2,1,128,1024]{2,0,1,3:T(2,128)}, u32[]{:S(2)}, u32[]{:S(2)}) async-start(f32[2,1,128,1024]{2,0,1,3:T(2,128)} %bitcast.926), calls=%async_computation.8 | async-start | bytes 2097152 | tf_op jit(solution)/shard_map/all_to_all | solution.py:151
  752.8 17.6 %collective-permute-start.23 = (f32[1,130,1024]{2,0,1:T(1,128)}, f32[1,130,1024]{2,0,1:T(1,128)}, u32[]{:S(2)}, u32[]{:S(2)}) collective-permute-start(f32[1,130,1024]{2,0,1:T(1,128)} %copy.501), channel_id=1, source_target_pairs={{1,0},{2,1},{3,2},{5,4},{6,5},{7,6},{9,8},{10,9},{11,10},{13,12},{... | collective-permute-start | bytes 1597448 | tf_op jit(solution)/shard_map/ppermute | solution.py:22
  754.1 18.0 %collective-permute-start.22 = (f32[1,130,1024]{2,0,1:T(1,128)}, f32[1,130,1024]{2,0,1:T(1,128)}, u32[]{:S(2)}, u32[]{:S(2)}) collective-permute-start(f32[1,130,1024]{2,0,1:T(1,128)} %copy.501), channel_id=1, source_target_pairs={{0,1},{1,2},{2,3},{4,5},{5,6},{6,7},{8,9},{9,10},{10,11},{12,13},{... | collective-permute-start | bytes 1597448 | tf_op jit(solution)/shard_map/ppermute | solution.py:21
  864.0 120.4 %all-to-all-start.10 = ((f32[2,1,128,1024]{2,0,1,3:T(2,128)}), f32[2,1,128,1024]{2,0,1,3:T(2,128)}, u32[]{:S(2)}, u32[]{:S(2)}) async-start(f32[2,1,128,1024]{2,0,1,3:T(2,128)} %bitcast.925), calls=%async_computation.10 | async-start | bytes 2097152 | tf_op jit(solution)/shard_map/all_to_all | solution.py:151
  (105 other events, 1487.0 us)
where the time goes:
time: 1000 us; the launch traced here: 989 us
  blocking collectives  267 us (27%)
  other arithmetic  188 us (19%)
  starting transfers between devices  170 us (17%)
  local copies, waits for them, and re-layouts  141 us (14%)
  waiting for transfers between devices  139 us (14%)
  matrix products  68.9 us (7%)
  between operations  16.5 us (2%)
    all_to_all x5, starting transfers between devices, inverse_transform(): lax.all_to_all(rows_part.reshape(2, batches, bins_here, groups * planes *...  79.1 us
    dot_general x44, matrix products, contract(): return jnp.einsum(form, left, table, precision=highest)  68.9 us
    all_to_all x5, waiting for transfers between devices, forward_fourier_map(): lax.all_to_all(across.reshape(2, batches, columns, planes * row_count), '...  55.8 us
    reduce_sum x2, other arithmetic, local(): jnp.sum(direction * applied)  54.3 us
    psum x1, blocking collectives, local(): norm_now = lax.psum(jnp.sum(right_side * right_side), ('gy', 'gz'))  52.7 us
    psum x1, blocking collectives, local(): lax.psum((jnp.sum(direction * applied), jnp.sum(upstream * direction)), (...  52.7 us
    ppermute x12, starting transfers between devices, extended(): before = lax.ppermute(last, axis, up)  52.4 us
    ppermute x12, waiting for transfers between devices, extended(): after = lax.ppermute(first, axis, down)  51.6 us
  transfers between devices with their start and end apart: 34, of which 23 were waited for; matrix products, arithmetic and copies ran while one was open for 17% of the time, Pallas kernels for 0%

commit v1 on v0

v1 whole, which is shorter than its diff:
```python
import math

import jax
import jax.numpy as jnp
from jax import lax
from jax.experimental import pallas as pl
from jax.experimental.pallas import tpu as pltpu
from jax.sharding import PartitionSpec as P

MESH = pl.DeviceIdType.MESH
SIDES = [(dy, dz) for dy in (-1, 0, 1) for dz in (-1, 0, 1) if (dy, dz) != (0, 0)]
VMEM = pl.BlockSpec(memory_space=pltpu.VMEM)
SMEM = pl.BlockSpec(memory_space=pltpu.SMEM)


def moved(value, shift):
    if shift == 0:
        return value
    width = value.shape[1]
    lane = lax.broadcasted_iota(jnp.int32, value.shape, 1)
    edge = 0 if shift > 0 else width - 1
    return jnp.where(lane == edge, 0.0, pltpu.roll(value, shift % width, 1))


def regular_kernel(count_y, count_z, weights, volume, back, grown, mapped, shifted, send, receive):
    rows, columns = volume.shape
    y, z = (lax.axis_index("gy"), lax.axis_index("gz"))

    def there(dy, dz):
        return (y + dy >= 0) & (y + dy < count_y) & (z + dz >= 0) & (z + dz < count_z)

    barrier = pltpu.get_barrier_semaphore()
    for dy, dz in SIDES:

        @pl.when(there(dy, dz))
        def _():
            pl.semaphore_signal(barrier, inc=1, device_id=(y + dy, z + dz), device_id_type=MESH)

    def span(place, count):
        return 1 + jnp.where(place > 0, 1, 0) + jnp.where(place < count - 1, 1, 0)

    pl.semaphore_wait(barrier, span(y, count_y) * span(z, count_z) - 1)

    def copy(field, phase, number):
        dy, dz = SIDES[number]
        source = field.at[1, pl.ds(rows if dy > 0 else 8, 8 if dy else rows)]
        start = 8 if dy == 0 else 0 if dy > 0 else rows + 8
        return pltpu.make_async_remote_copy(
            src_ref=source,
            dst_ref=field.at[1 - dz, pl.ds(start, 8 if dy else rows)],
            send_sem=send.at[phase, number],
            recv_sem=receive.at[phase, number],
            device_id=(y + dy, z + dz),
            device_id_type=MESH,
        )

    def exchange(field, phase):
        for number, (dy, dz) in enumerate(SIDES):

            @pl.when(there(dy, dz))
            def _():
                copy(field, phase, number).start()

        for number, (dy, dz) in enumerate(SIDES):
            start = 8 if dy == 0 else 0 if dy > 0 else rows + 8

            @pl.when(jnp.logical_not(there(-dy, -dz)))
            def _():
                field[1 - dz, pl.ds(start, 8 if dy else rows)] = jnp.zeros(
                    (8 if dy else rows, columns), jnp.float32
                )

        for number, (dy, dz) in enumerate(SIDES):

            @pl.when(there(-dy, -dz))
            def _():
                copy(field, phase, number).wait_recv()

            @pl.when(there(dy, dz))
            def _():
                copy(field, phase, number).wait_send()

    def apply(field, flip, put):
        def weight(a, b, c):
            return weights[26 - (9 * a + 3 * b + c) if flip else 9 * a + 3 * b + c]

        @pl.loop(0, (rows + 16) // 8)
        def _(step):
            here = pl.ds(pl.multiple_of(step * 8, 8), 8)
            sums = [None] * 3
            for a in range(3):
                value = field[a, here]
                for c in range(3):
                    turned = moved(value, 1 - c)
                    for b in range(3):
                        term = weight(a, b, c) * turned
                        sums[b] = term if sums[b] is None else sums[b] + term
            for b in range(3):
                shifted[b, here] = sums[b]

        @pl.loop(0, rows // 8)
        def _(step):
            first = pl.multiple_of(step * 8, 8)
            around = pl.ds(first, 24)
            total = shifted[1, pl.ds(first + 8, 8)]
            total = total + shifted[0, around][7:15] + shifted[2, around][9:17]
            put(first, total)

    @pl.loop(0, rows // 8)
    def _(step):
        first = pl.multiple_of(step * 8, 8)
        grown[1, pl.ds(first + 8, 8)] = volume[pl.ds(first, 8)]

    exchange(grown, 0)

    def put_mapped(first, total):
        mapped[1, pl.ds(first + 8, 8)] = total

    apply(grown, False, put_mapped)
    exchange(mapped, 1)

    def put_back(first, total):
        back[pl.ds(first, 8)] = total

    apply(mapped, True, put_back)


def regular(volume, kernel):
    rows, columns = volume.shape[1:]
    count_y, count_z = (lax.axis_size("gy"), lax.axis_size("gz"))
    field = jax.ShapeDtypeStruct((3, rows + 16, columns), jnp.float32)

    def body(*refs):
        regular_kernel(count_y, count_z, *refs)

    back, grown, mapped = pl.pallas_call(
        body,
        out_shape=(jax.ShapeDtypeStruct((rows, columns), jnp.float32), field, field),
        in_specs=[SMEM, VMEM],
        out_specs=(VMEM, VMEM, VMEM),
        scratch_shapes=[
            pltpu.VMEM((3, rows + 16, columns), jnp.float32),
            pltpu.SemaphoreType.DMA((2, 8)),
            pltpu.SemaphoreType.DMA((2, 8)),
        ],
        cost_estimate=pl.CostEstimate(flops=120 * rows * columns, bytes_accessed=20 * rows * columns, transcendentals=0),
        compiler_params=pltpu.CompilerParams(collective_id=0, has_side_effects=True),
        name="regular",
    )(kernel.reshape(27), volume[0])
    return (back[None], grown, mapped)


def total_kernel(count_y, count_z, value, out, column, row, across, send, receive):
    y, z = (lax.axis_index("gy"), lax.axis_index("gz"))
    along_y = [(lax.rem(y + k, count_y), z) for k in range(1, count_y)]
    along_z = [(y, lax.rem(z + k, count_z)) for k in range(1, count_z)]
    barrier = pltpu.get_barrier_semaphore()
    for place in along_y + along_z:
        pl.semaphore_signal(barrier, inc=1, device_id=place, device_id_type=MESH)
    pl.semaphore_wait(barrier, count_y + count_z - 2)

    def gather(source, slots, places, base):
        copies = []
        for k, place in enumerate(places):
            copies.append(
                pltpu.make_async_remote_copy(
                    src_ref=source,
                    dst_ref=slots.at[k],
                    send_sem=send.at[base + k],
                    recv_sem=receive.at[base + k],
                    device_id=place,
                    device_id_type=MESH,
                )
            )
            copies[-1].start()
        for item in copies:
            item.wait()

    def ordered(own, slots, index, count):
        total = jnp.zeros_like(own)
        for j in range(count):
            term = own
            for k in range(1, count):
                term = jnp.where(lax.rem(index - j + count, count) == k, slots[k - 1], term)
            total = total + term
        return total

    gather(value, column, along_y, 0)
    across[...] = ordered(value[...], column, y, count_y)
    gather(across, row, along_z, count_y - 1)
    out[...] = ordered(across[...], row, z, count_z)


def total(values, collective):
    count_y, count_z = (lax.axis_size("gy"), lax.axis_size("gz"))
    count = values.shape[0]

    def body(*refs):
        total_kernel(count_y, count_z, *refs)

    block = jnp.broadcast_to(jnp.pad(values, (0, 128 - count))[None], (8, 128))
    copies = count_y + count_z - 2
    summed = pl.pallas_call(
        body,
        out_shape=jax.ShapeDtypeStruct((8, 128), jnp.float32),
        in_specs=[VMEM],
        out_specs=VMEM,
        scratch_shapes=[
            pltpu.VMEM((count_y - 1, 8, 128), jnp.float32),
            pltpu.VMEM((count_z - 1, 8, 128), jnp.float32),
            pltpu.VMEM((8, 128), jnp.float32),
            pltpu.SemaphoreType.DMA((copies,)),
            pltpu.SemaphoreType.DMA((copies,)),
        ],
        compiler_params=pltpu.CompilerParams(collective_id=collective, has_side_effects=True),
        name="total",
    )(block)
    return summed[0, :count]


def correlate_kernel(scalars, grown_0, grown_1, grown_2, grown_up, mapped_0, mapped_1, mapped_2, mapped_up, out):
    rows = grown_0.shape[1] - 16
    columns = grown_0.shape[2]
    c_up, c_zero, c_one, c_two, d_zero, d_one, s_zero, s_grad, s_direction = (scalars[k] for k in range(9))
    out[...] = jnp.zeros_like(out)

    @pl.loop(0, rows // 8)
    def _(step):
        first = pl.multiple_of(step * 8, 8)
        here = pl.ds(first + 8, 8)
        zero, one = (mapped_0[1, here], mapped_1[1, here])
        grad = c_up * mapped_up[1, here] + c_zero * zero + c_one * one + c_two * mapped_2[1, here]
        values = (
            s_zero * zero + s_grad * grad,
            s_grad * zero,
            s_direction * (d_zero * zero + d_one * one),
        )
        turned = [[moved(value, c - 1) for value in values] for c in range(3)]
        for a in range(3):
            around = pl.ds(first, 24)
            full_0, full_1 = (grown_0[a, around], grown_1[a, around])
            full_grad = c_up * grown_up[a, around] + c_zero * full_0 + c_one * full_1 + c_two * grown_2[a, around]
            full_direction = d_zero * full_0 + d_one * full_1
            for b in range(3):
                fields = [item[7 + b : 15 + b] for item in (full_0, full_grad, full_direction)]
                for c in range(3):
                    product = turned[c][0] * fields[0] + turned[c][1] * fields[1] + turned[c][2] * fields[2]
                    folded = product[:, :128]
                    for part in range(1, columns // 128):
                        folded = folded + product[:, 128 * part : 128 * part + 128]
                    out[9 * a + 3 * b + c] += folded


def correlate(scalars, *fields):
    return pl.pallas_call(
        correlate_kernel,
        out_shape=jax.ShapeDtypeStruct((27, 8, 128), jnp.float32),
        in_specs=[SMEM] + [VMEM] * 8,
        out_specs=VMEM,
        cost_estimate=pl.CostEstimate(flops=40000000, bytes_accessed=8000000, transcendentals=0),
        name="correlate",
    )(scalars, *fields).sum((1, 2))


def contract(form, left, right):
    return jnp.einsum(form, left, right, precision=lax.Precision.HIGH)


def wave_tables(length, groups):
    half = length // 2
    bins = half // groups
    pair = groups // 2
    shape = (half, pair, 2, bins)
    place = lax.broadcasted_iota(jnp.int32, shape, 0)
    part = lax.broadcasted_iota(jnp.int32, shape, 2)
    slot = lax.broadcasted_iota(jnp.int32, shape, 1) * bins + lax.broadcasted_iota(jnp.int32, shape, 3)
    tables = []
    for odd in range(2):
        frequency = 2 * slot + odd
        steps = place * frequency + part * (length // 4)
        if not odd:
            steps = jnp.where((slot == 0) & (part == 1), place * half, steps)
        angle = (steps % length).astype(jnp.float32) * (2.0 * math.pi / length)
        tables.append(jnp.cos(angle).reshape(half, pair, 2 * bins))
    return tables


def combine(raw, on_row, on_lane):
    even, odd = raw
    a, b, c, d = (
        jnp.concatenate([piece[:, part, :, :, side] for piece in (even, odd)], 0)
        for part, side in ((0, 0), (0, 1), (1, 0), (1, 1))
    )
    special = on_row | on_lane
    plus_real = jnp.where(special, a, a - d)
    plus_imaginary = jnp.where(on_row, b, jnp.where(on_lane, c, b + c))
    minus_real = jnp.where(on_row, c, jnp.where(on_lane, b, a + d))
    minus_imaginary = jnp.where(special, d, b - c)
    return (jnp.stack([plus_real, minus_real]), jnp.stack([plus_imaginary, minus_imaginary]))


def separate(spectrum, on_row, on_lane):
    (plus_real, minus_real), (plus_imaginary, minus_imaginary) = spectrum
    special = on_row | on_lane
    a = jnp.where(special, plus_real, plus_real + minus_real)
    d = jnp.where(special, minus_imaginary, minus_real - plus_real)
    b = jnp.where(on_row, plus_imaginary, jnp.where(on_lane, minus_real, plus_imaginary + minus_imaginary))
    c = jnp.where(on_row, minus_real, jnp.where(on_lane, plus_imaginary, plus_imaginary - minus_imaginary))
    scale = jnp.where(on_row & on_lane, 1.0, 2.0)
    a, b, c, d = (value * scale for value in (a, b, c, d))
    whole = jnp.stack([jnp.stack([a, b], 3), jnp.stack([c, d], 3)], 1)
    pair = whole.shape[0] // 2
    return (whole[:pair], whole[pair:])


def times(left, right, corner, conjugate=False):
    (a, b), (c, d) = (left, right)
    cross = b * d
    sign = -1.0 if conjugate else 1.0
    real = jnp.where(corner, a * c, a * c - sign * cross)
    imaginary = jnp.where(corner, cross, sign * a * d + b * c)
    return (real, imaginary)


def linear(*terms):
    total_real = total_imaginary = 0.0
    for scale, (real, imaginary) in terms:
        scale_real, scale_imaginary = scale if isinstance(scale, tuple) else (scale, scale)
        total_real = total_real + scale_real * real
        total_imaginary = total_imaginary + scale_imaginary * imaginary
    return (total_real, total_imaginary)


def local(measured, point_spread, stencil_weights, upstream):
    planes, row_count, columns = measured.shape
    groups = lax.axis_size("gy")
    rows = row_count * groups
    cells = planes * rows * columns * lax.axis_size("gz")
    bins = columns // 2 // groups
    even_x, odd_x = wave_tables(columns, groups)
    even_y, odd_y = (even_x, odd_x) if rows == columns else wave_tables(rows, groups)
    y_bins = rows // 2 // groups
    spectral = (groups, y_bins, 1, bins)
    on_row = (lax.broadcasted_iota(jnp.int32, spectral, 0) == 0) & (
        lax.broadcasted_iota(jnp.int32, spectral, 1) == 0
    )
    on_lane = (lax.broadcasted_iota(jnp.int32, spectral, 3) == 0) & (lax.axis_index("gy") == 0)
    corner = on_row & on_lane

    def forward(volumes):
        count = volumes.shape[0]
        low, high = (volumes[:, :, : columns // 2], volumes[:, :, columns // 2 :])
        sent = jnp.concatenate(
            [contract("vrj,jdl->drvl", low + high, even_x), contract("vrj,jdl->drvl", low - high, odd_x)], 0
        )
        arrived = lax.all_to_all(
            sent.reshape(groups, row_count, count * 2 * bins), "gy", split_axis=0, concat_axis=0, tiled=True
        )
        arrived = arrived.reshape(rows, count * 2 * bins)
        low, high = (arrived[: rows // 2], arrived[rows // 2 :])
        raw = [
            contract("jds,jl->dsl", table, value).reshape(groups // 2, 2, y_bins, count, 2, bins)
            for table, value in ((even_y, low + high), (odd_y, low - high))
        ]
        return combine(raw, on_row, on_lane)

    def inverse(spectrum):
        count = spectrum[0].shape[3]
        pieces = separate(spectrum, on_row, on_lane)
        one, two = (
            contract("jds,dsl->jl", table, piece.reshape(groups // 2, 2 * y_bins, count * 2 * bins))
            for table, piece in ((even_y, pieces[0]), (odd_y, pieces[1]))
        )
        sent = jnp.concatenate([one + two, one - two], 0).reshape(groups, row_count, count * 2 * bins)
        arrived = lax.all_to_all(sent, "gy", split_axis=0, concat_axis=0, tiled=True)
        arrived = arrived.reshape(groups, row_count, count, 2 * bins)
        one = contract("drvl,jdl->vrj", arrived[: groups // 2], even_x)
        two = contract("drvl,jdl->vrj", arrived[groups // 2 :], odd_x)
        return jnp.concatenate([one + two, one - two], 2) / float(rows * columns)

    def pick(spectrum, start, count):
        return tuple(lax.slice_in_dim(part, start, start + count, axis=3) for part in spectrum)

    def join(*spectra):
        return tuple(jnp.concatenate(parts, 3) for parts in zip(*spectra))

    spectra = forward(jnp.concatenate([point_spread[None], measured], 0))
    transfer = pick(spectra, 0, 1)
    squares = (transfer[0] ** 2, transfer[1] ** 2)
    gain = (
        jnp.where(corner, squares[0], squares[0] + squares[1]),
        jnp.where(corner, squares[1], squares[0] + squares[1]),
    )
    spectrum_0 = times(pick(spectra, 1, planes), transfer, corner, True)
    blurred_0 = linear((gain, spectrum_0))
    pair = inverse(join(spectrum_0, blurred_0))
    vector_0 = pair[:planes]
    back_0, grown_0, mapped_0 = regular(vector_0, stencil_weights)
    back_up, grown_up, mapped_up = regular(upstream, stencil_weights)
    vector_1 = pair[planes:] + back_0
    spectrum_1 = linear((1.0, blurred_0), (1.0, forward(back_0)))
    blurred_1 = linear((gain, spectrum_1))
    early = forward(jnp.concatenate([upstream, back_up], 0))
    back_1, grown_1, mapped_1 = regular(vector_1, stencil_weights)
    vector_2 = inverse(blurred_1) + back_1
    norm_0, curve_0, image_0, up_0, up_1 = total(
        jnp.stack(
            [
                jnp.sum(vector_0 * vector_0),
                jnp.sum(vector_0 * vector_1),
                jnp.sum(vector_1 * vector_1),
                jnp.sum(upstream * vector_0),
                jnp.sum(upstream * vector_1),
            ]
        ),
        1,
    )
    step_0 = norm_0 / curve_0
    residual = vector_0 - step_0 * vector_1
    residual_image = vector_1 - step_0 * vector_2
    norm_1, cross, inner, up_residual, image_cross = total(
        jnp.stack(
            [
                jnp.sum(residual * residual),
                jnp.sum(residual * vector_1),
                jnp.sum(residual * residual_image),
                jnp.sum(upstream * residual),
                jnp.sum(residual_image * vector_1),
            ]
        ),
        2,
    )
    back_2, grown_2, mapped_2 = regular(vector_2, stencil_weights)
    late = forward(jnp.concatenate([back_1, back_2], 0))
    ratio = norm_1 / norm_0
    curve_1 = inner + 2.0 * ratio * cross + ratio * ratio * curve_0
    step_1 = norm_1 / curve_1
    grad_step_1 = up_residual + ratio * up_0
    grad_curve_1 = -grad_step_1 * step_1 / curve_1
    grad_ratio = step_1 * up_0 + 2.0 * grad_curve_1 * (cross + ratio * curve_0)
    known_image = step_1 * up_1 + 2.0 * grad_curve_1 * (image_cross + ratio * image_0)
    grad_norm = grad_step_1 / curve_1 + grad_ratio / norm_0
    grad_step_0 = up_0 - known_image - 2.0 * grad_norm * cross
    grad_curve_0 = -grad_step_0 * step_0 / curve_0
    grad_norm_0 = -grad_ratio * ratio / norm_0 + grad_step_0 / curve_0

    spectrum_2 = linear((1.0, linear((gain, spectrum_1))), (1.0, pick(late, 0, planes)))
    spectrum_up = pick(early, 0, planes)
    residual_terms = ((1.0, spectrum_0), (-step_0, spectrum_1))
    direction_image = linear((1.0 + ratio, spectrum_1), (-step_0, spectrum_2))
    grad_direction = linear((step_1, spectrum_up), (2.0 * grad_curve_1, direction_image))
    grad_residual = linear((1.0, grad_direction), (2.0 * grad_norm, linear(*residual_terms)))
    grad_back = linear(
        (step_1, pick(early, planes, planes)),
        (2.0 * grad_curve_1 * (1.0 + ratio) - 2.0 * grad_norm * step_0, pick(late, 0, planes)),
        (-2.0 * grad_curve_1 * step_0, pick(late, planes, planes)),
        (2.0 * grad_norm, linear((1.0, spectrum_1), (-1.0, blurred_0))),
    )
    grad_right = linear(
        (step_0, spectrum_up),
        (ratio, grad_direction),
        (2.0 * grad_curve_0, spectrum_1),
        (2.0 * grad_norm_0, spectrum_0),
        (1.0, grad_residual),
        (-step_0, linear((gain, grad_residual), (1.0, grad_back))),
    )
    grad_measured = inverse(times(grad_right, transfer, corner))

    terms = correlate(
        jnp.stack(
            [
                step_1,
                2.0 * grad_norm,
                2.0 * grad_curve_1 * (1.0 + ratio) - 2.0 * grad_norm * step_0,
                -2.0 * grad_curve_1 * step_0,
                1.0 + ratio,
                -step_0,
                2.0 * grad_curve_0,
                -step_0,
                2.0 * grad_curve_1,
            ]
        ),
        grown_0, grown_1, grown_2, grown_up, mapped_0, mapped_1, mapped_2, mapped_up,
    )
    grad_stencil = total(terms, 3).reshape(3, 3, 3) / math.sqrt(cells)
    return (grad_measured, grad_stencil)


def solution(mesh):
    return jax.shard_map(
        local,
        mesh=mesh,
        in_specs=(P("gz", "gy", None), P("gy", None), P(), P("gz", "gy", None)),
        out_specs=(P("gz", "gy", None), P()),
        check_vma=False,
    )
```

time: 1000 us -> 653 us (0.65)
  Pallas kernels: 0 us -> 276 us
  blocking collectives: 267 us -> 0 us
  other arithmetic: 188 us -> 41.7 us
  starting transfers between devices: 170 us -> 66.7 us
  waiting for transfers between devices: 139 us -> 57.9 us
  local copies, waits for them, and re-layouts: 141 us -> 62.9 us
  matrix products: 68.9 us -> 121 us
    pallas_call x0 -> x8, Pallas kernels: none -> 276 us  [the longest x4 212 us: regular(): pl.pallas_call(body, out_shape=(jax.ShapeDtypeStruct((rows, columns), jnp...]
    psum x5 -> x0, blocking collectives: 234 us -> none  [the longest x1 52.7 us: local(): norm_now = lax.psum(jnp.sum(right_side * right_side), ('gy', 'gz'))]
    reduce_sum x10 -> x3, other arithmetic: 99.8 us -> 6.2 us  [the longest x1 3.24 us: local(): jnp.sum(upstream * vector_0)]
    ppermute x24 -> x0, starting transfers between devices: 67.9 us -> none  [the longest x12 52.4 us: extended(): before = lax.ppermute(last, axis, up)]
    another operation x13 -> x5, local copies, waits for them, and re-layouts: 70.1 us -> 11.2 us  [the longest x1 3.74 us: local(): jnp.stack([jnp.sum(residual * residual), jnp.sum(residual * vector_1), jn...]
    ppermute x24 -> x0, waiting for transfers between devices: 56.4 us -> none  [the longest x12 51.6 us: extended(): after = lax.ppermute(first, axis, down)]
    dot_general x44 -> x28, matrix products: 68.9 us -> 121 us  [contract(): return jnp.einsum(form, left, right, precision=lax.Precision.HIGH)]
    all_to_all x10 -> x7, starting transfers between devices: 102 us -> 66.7 us  [the longest x4 55.3 us: forward(): lax.all_to_all(sent.reshape(groups, row_count, count * 2 * bins), 'gy', s...]
  transfers between devices with their start and end apart: 34 -> 7, of which waited for: 23 -> 3; matrix products, arithmetic and copies ran while one was open for 17% -> 13% of each run, Pallas kernels for 0% -> 35%
where the time goes in v1:
time: 653 us; the launch traced here: 643 us
  Pallas kernels  276 us (42%)
  matrix products  121 us (19%)
  starting transfers between devices  66.7 us (10%)
  local copies, waits for them, and re-layouts  62.9 us (10%)
  waiting for transfers between devices  57.9 us (9%)
  other arithmetic  41.7 us (6%)
  between operations  17 us (3%)
    pallas_call x4, Pallas kernels, regular(): pl.pallas_call(body, out_shape=(jax.ShapeDtypeStruct((rows, columns), jnp...  212 us
    dot_general x28, matrix products, contract(): return jnp.einsum(form, left, right, precision=lax.Precision.HIGH)  121 us
    all_to_all x4, starting transfers between devices, forward(): lax.all_to_all(sent.reshape(groups, row_count, count * 2 * bins), 'gy', s...  55.3 us
    pallas_call x3, Pallas kernels, total(): pl.pallas_call(body, out_shape=jax.ShapeDtypeStruct((8, 128), jnp.float32...  51.6 us
    all_to_all x4, waiting for transfers between devices, forward(): lax.all_to_all(sent.reshape(groups, row_count, count * 2 * bins), 'gy', s...  32 us
    all_to_all x3, waiting for transfers between devices, inverse(): lax.all_to_all(sent, 'gy', split_axis=0, concat_axis=0, tiled=True)  25.9 us
  transfers between devices with their start and end apart: 7, of which 3 were waited for; matrix products, arithmetic and copies ran while one was open for 13% of the time, Pallas kernels for 35%

profile of v1, /device:TPU:0, one launch (start us, length us, event | category | flops | bytes accessed | tf_op | source)
XLA Modules:
  0.0 642.9 jit_solution(5269032823555812526)
XLA Ops:
  1.1 6.0 convolution_bitcast_fusion.10
  13.5 6.5 %all-to-all-start = ((f32[8,128,256]{2,1,0:T(8,128)}), f32[8,128,256]{2,1,0:T(8,128)S(1)}, u32[]{:S(2)}, u32[]{:S(2)}) async-start(f32[8,128,256]{2,1,0:T(8,128)} %copy.150), calls=%async_computation | async-start | bytes 2097152 | tf_op jit(solution)/shard_map/all_to_all | solution.py:356
  24.3 22.1 %all-to-all-done = f32[8,128,256]{2,1,0:T(8,128)S(1)} async-done(((f32[8,128,256]{2,1,0:T(8,128)}), f32[8,128,256]{2,1,0:T(8,128)S(1)}, u32[]{:S(2)}, u32[]{:S(2)}) %all-to-all-start) | async-done | bytes 1048608 | tf_op jit(solution)/shard_map/all_to_all | solution.py:356
  52.0 5.8 fusion.30
  66.3 6.4 convolution_bitcast_fusion.8
  75.1 5.9 fusion.269
  86.6 25.9 %all-to-all-done.1 = f32[8,128,256]{1,2,0:T(8,128)S(1)} async-done(((f32[8,128,256]{1,2,0:T(8,128)}), f32[8,128,256]{1,2,0:T(8,128)S(1)}, u32[]{:S(2)}, u32[]{:S(2)}) %all-to-all-start.1) | async-done | bytes 1048608 | tf_op jit(solution)/shard_map/all_to_all | solution.py:375
  123.8 49.7 %regular.4 = (f32[128,1024]{1,0:T(8,128)}, f32[3,144,1024]{2,1,0:T(8,128)}, f32[3,144,1024]{2,1,0:T(8,128)}) custom-call(f32[27]{0:T(128)} %reshape.2572.refs_0_, f32[128,1024]{1,0:T(8,128)} %slice_bitcast_fusion.refs_1_), custom_call_target="tpu_custom_call" | custom-call | flops 15728640 | bytes 2621440 | tf_op jit(solution)/shard_map/regular/pallas_call | solution.py:136
  173.5 5.9 convolution_bitcast_fusion.21
  185.1 14.1 %all-to-all-start.3 = ((f32[8,128,128]{1,2,0:T(8,128)}), f32[8,128,128]{1,2,0:T(8,128)}, u32[]{:S(2)}, u32[]{:S(2)}) async-start(f32[8,128,128]{1,2,0:T(8,128)} %maximum_bitcast_fusion.2), calls=%async_computation.3 | async-start | bytes 1048576 | tf_op jit(solution)/shard_map/all_to_all | solution.py:356
  204.7 9.9 %all-to-all-done.3 = f32[8,128,128]{1,2,0:T(8,128)} async-done(((f32[8,128,128]{1,2,0:T(8,128)}), f32[8,128,128]{1,2,0:T(8,128)}, u32[]{:S(2)}, u32[]{:S(2)}) %all-to-all-start.3) | async-done | bytes 524320 | tf_op jit(solution)/shard_map/all_to_all | solution.py:356
  232.2 6.1 convolution_bitcast_fusion.18
  241.6 5.7 fusion.273
  252.3 52.1 %regular.5 = (f32[128,1024]{1,0:T(8,128)}, f32[3,144,1024]{2,1,0:T(8,128)}, f32[3,144,1024]{2,1,0:T(8,128)}) custom-call(f32[27]{0:T(128)} %reshape.2572.refs_0_, f32[128,1024]{1,0:T(8,128)} %bitcast.518), custom_call_target="tpu_custom_call" | custom-call | flops 15728640 | bytes 2621440 | tf_op jit(solution)/shard_map/regular/pallas_call | solution.py:136
  304.4 6.0 convolution_bitcast_fusion.6
  319.0 17.3 %all-to-all-start.2 = ((f32[8,128,256]{2,1,0:T(8,128)}), f32[8,128,256]{2,1,0:T(8,128)}, u32[]{:S(2)}, u32[]{:S(2)}) async-start(f32[8,128,256]{2,1,0:T(8,128)} %copy.183), calls=%async_computation.2 | async-start | bytes 2097152 | tf_op jit(solution)/shard_map/all_to_all | solution.py:356
  344.4 24.5 %total.3 = f32[8,128]{1,0:T(8,128)} custom-call(f32[8,128]{1,0:T(8,128)} %broadcast_in_dim.168.refs_0_), custom_call_target="tpu_custom_call" | custom-call | tf_op jit(solution)/shard_map/total/pallas_call | solution.py:203
  371.8 48.6 %regular.6 = (f32[128,1024]{1,0:T(8,128)}, f32[3,144,1024]{2,1,0:T(8,128)}, f32[3,144,1024]{2,1,0:T(8,128)}) custom-call(f32[27]{0:T(128)} %reshape.2572.refs_0_, f32[128,1024]{1,0:T(8,128)} %bitcast.519), custom_call_target="tpu_custom_call" | custom-call | flops 15728640 | bytes 2621440 | tf_op jit(solution)/shard_map/regular/pallas_call | solution.py:136
  433.4 62.1 %regular.7 = (f32[128,1024]{1,0:T(8,128)}, f32[3,144,1024]{2,1,0:T(8,128)}, f32[3,144,1024]{2,1,0:T(8,128)}) custom-call(f32[27]{0:T(128)} %reshape.2572.refs_0_, f32[128,1024]{1,0:T(8,128)} %get-tuple-element.45.refs_1_), custom_call_target="tpu_custom_call" | custom-call | flops 15728640 | bytes 2621440 | tf_op jit(solution)/shard_map/regular/pallas_call | solution.py:136
  495.6 6.0 convolution_bitcast_fusion.2
  510.1 17.3 %all-to-all-start.5 = ((f32[8,128,256]{2,1,0:T(8,128)}), f32[8,128,256]{2,1,0:T(8,128)}, u32[]{:S(2)}, u32[]{:S(2)}) async-start(f32[8,128,256]{2,1,0:T(8,128)} %copy.210), calls=%async_computation.5 | async-start | bytes 2097152 | tf_op jit(solution)/shard_map/all_to_all | solution.py:356
  544.4 15.6 %total.4 = f32[8,128]{1,0:T(8,128)} custom-call(f32[8,128]{1,0:T(8,128)} %broadcast_in_dim.172.refs_0_), custom_call_target="tpu_custom_call" | custom-call | tf_op jit(solution)/shard_map/total/pallas_call | solution.py:203
  606.1 11.9 %correlate.1 = f32[27,8,128]{2,1,0:T(8,128)} custom-call(f32[9]{0:T(128)} %stack.204.scalars, f32[3,144,1024]{2,1,0:T(8,128)} %get-tuple-element.18.grown_0, f32[3,144,1024]{2,1,0:T(8,128)} %get-tuple-element.19.grown_1, f32[3,144,1024]{2,1,0:T(8,128)} %get-tuple-element.20.grown_2, f32[3,144,1024]{2,1,0:T(8,128)} %get-tuple-element.21.grown_up, ...), custom_call_target="tpu_custom_call" | custom-call | flops 40000000 | bytes 8000000 | tf_op jit(solution)/shard_map/correlate/pallas_call | solution.py:255
  619.8 11.4 %total.5 = f32[8,128]{1,0:T(8,128)} custom-call(f32[8,128]{1,0:T(8,128)} %broadcast_in_dim.175.refs_0_), custom_call_target="tpu_custom_call" | custom-call | tf_op jit(solution)/shard_map/total/pallas_call | solution.py:203
  (312 shorter events, 183.1 us)
Async XLA Ops:
  0.6 198.6 %copy-start.62 = (s32[4]{0:T(128)}, s32[4]{0:T(128)S(1)}, u32[]{:S(2)}) copy-start(s32[4]{0:T(128)S(1)} %iota_multiply_fusion.3) | copy-start | bytes 52
  0.7 198.6 %copy-start.57 = (s32[512]{0:T(512)}, s32[512]{0:T(512)S(1)}, u32[]{:S(2)}) copy-start(s32[512]{0:T(512)S(1)} %get-tuple-element.165) | copy-start | bytes 6148
  0.8 178.6 %copy-start.67 = (s32[128]{0:T(128)}, s32[128]{0:T(128)S(1)}, u32[]{:S(2)}) copy-start(s32[128]{0:T(128)S(1)} %iota.818) | copy-start | bytes 1540
  0.9 178.5 %copy-start.72 = (s32[128]{0:T(128)}, s32[128]{0:T(128)S(1)}, u32[]{:S(2)}) copy-start(s32[128]{0:T(128)S(1)} %iota.809) | copy-start | bytes 1540
  1.1 172.4 %copy-start.81 = (pred[128]{0:T(512)(128)(4,1)}, pred[128]{0:T(512)(128)(4,1)S(1)}, u32[]{:S(2)}) copy-start(pred[128]{0:T(512)(128)(4,1)S(1)} %iota.813) | copy-start | bytes 388
  13.5 32.9 %all-to-all-start = ((f32[8,128,256]{2,1,0:T(8,128)}), f32[8,128,256]{2,1,0:T(8,128)S(1)}, u32[]{:S(2)}, u32[]{:S(2)}) async-start(f32[8,128,256]{2,1,0:T(8,128)} %copy.150), calls=%async_computation | async-start | bytes 2097152 | tf_op jit(solution)/shard_map/all_to_all | solution.py:356
  20.2 40.0 %copy-start.47 = (pred[8,64,64]{2,1,0:T(8,128)(4,1)}, pred[8,64,64]{2,1,0:T(8,128)(4,1)S(1)}, u32[]{:S(2)}) copy-start(pred[8,64,64]{2,1,0:T(8,128)(4,1)S(1)} %get-tuple-element.156) | copy-start | bytes 98308
  66.3 6.4 copy-start.17
  82.4 30.1 %all-to-all-start.1 = ((f32[8,128,256]{1,2,0:T(8,128)}), f32[8,128,256]{1,2,0:T(8,128)S(1)}, u32[]{:S(2)}, u32[]{:S(2)}) async-start(f32[8,128,256]{1,2,0:T(8,128)} %copy.174), calls=%async_computation.1 | async-start | bytes 2097152 | tf_op jit(solution)/shard_map/all_to_all | solution.py:375
  185.1 29.6 %all-to-all-start.3 = ((f32[8,128,128]{1,2,0:T(8,128)}), f32[8,128,128]{1,2,0:T(8,128)}, u32[]{:S(2)}, u32[]{:S(2)}) async-start(f32[8,128,128]{1,2,0:T(8,128)} %maximum_bitcast_fusion.2), calls=%async_computation.3 | async-start | bytes 1048576 | tf_op jit(solution)/shard_map/all_to_all | solution.py:356
  232.2 6.2 copy-start.46
  248.1 70.9 %all-to-all-start.4 = ((f32[8,128,128]{2,1,0:T(8,128)}), f32[8,128,128]{2,1,0:T(8,128)}, u32[]{:S(2)}, u32[]{:S(2)}) async-start(f32[8,128,128]{2,1,0:T(8,128)} %bitcast.533), calls=%async_computation.4 | async-start | bytes 1048576 | tf_op jit(solution)/shard_map/all_to_all | solution.py:375
  304.4 6.1 copy-start.14
  304.4 6.1 copy-start.58
  319.0 191.1 %all-to-all-start.2 = ((f32[8,128,256]{2,1,0:T(8,128)}), f32[8,128,256]{2,1,0:T(8,128)}, u32[]{:S(2)}, u32[]{:S(2)}) async-start(f32[8,128,256]{2,1,0:T(8,128)} %copy.183), calls=%async_computation.2 | async-start | bytes 2097152 | tf_op jit(solution)/shard_map/all_to_all | solution.py:356
  495.5 6.1 copy-start.56
  495.5 6.1 copy-start.59
  495.5 6.1 copy-start.65
  495.5 6.1 copy-start.70
  495.5 6.1 copy-start.75
  495.6 6.1 copy-start.79
  495.6 6.1 copy-start.83
  510.1 64.3 %all-to-all-start.5 = ((f32[8,128,256]{2,1,0:T(8,128)}), f32[8,128,256]{2,1,0:T(8,128)}, u32[]{:S(2)}, u32[]{:S(2)}) async-start(f32[8,128,256]{2,1,0:T(8,128)} %copy.210), calls=%async_computation.5 | async-start | bytes 2097152 | tf_op jit(solution)/shard_map/all_to_all | solution.py:356
  601.7 30.9 %all-to-all-start.6 = ((f32[8,128,128]{2,1,0:T(8,128)}), f32[8,128,128]{2,1,0:T(8,128)S(1)}, u32[]{:S(2)}, u32[]{:S(2)}) async-start(f32[8,128,128]{2,1,0:T(8,128)} %bitcast.197), calls=%async_computation.6 | async-start | bytes 1048576 | tf_op jit(solution)/shard_map/all_to_all | solution.py:375
  (68 other events, 157.5 us)
